TPU v7x, 512 devices: a whole 4x4x16 slice. The times are simulated.
512 devices in a mesh: gy: 16 (over x_hi, y, core), gx: 32 (over z, x_lo).
Axes of the slice: x: 4 (x_hi: 2, x_lo: 2; x = x_hi * 2 + x_lo), y: 4, z: 16, core: 2. Of those that a mesh axis runs over, the one named last changes fastest.
Arguments:
- embeddings: bfloat16 [128, 4096, 128], P('gy', 'gx'), may hold values from -180 to 180
- affinity: float32 [4, 128, 4096], P(None, 'gy', 'gx'), may hold values from 0 to 1, as said below
- assignment: int32 [128, 4096], P('gy', 'gx'), may hold values from 0 to 1023
Outputs:
- min_distance: float32 [128, 4096], P('gy', 'gx')
- new_centroids: float32 [1024, 128], replicated
Inputs may be any that keep to these rules, and one draw needn't show every extreme that they name: `affinity`: weight 0 exactly for edges that leave the slab; every other edge weighs 0.05 or more.
All inputs are finite; a program needn't handle non-finite values.
Results may differ from a plain program's by a relative error of at most 0.00045.
Values may be sent and summed in bfloat16 or wider, within the bound.
No kernel may reach another device: no remote copies, remote signals or barrier semaphores. Data moves between devices by JAX's collectives and lax.ppermute only.
A program may use at most 64 MiB of HBM per device.

v0:
```python
import math
import jax
import jax.numpy as jnp
from jax import lax
from jax.sharding import PartitionSpec as P

K = 1024
DEGREE = 4
COEFFS = (0.5, 0.45, 0.35, 0.25, 0.15)


def extended(block, sides, width):
    for axis, dim in sides:
        count = lax.axis_size(axis)
        forward = [(i, i + 1) for i in range(count - 1)]
        backward = [(target, source) for source, target in forward]
        low = lax.ppermute(
            lax.slice_in_dim(block, block.shape[dim] - width, None, axis=dim), axis, forward
        )
        high = lax.ppermute(lax.slice_in_dim(block, 0, width, axis=dim), axis, backward)
        block = jnp.concatenate([low, block, high], axis=dim)
    return block


def degree_of(w_ext):
    w_east, w_south, w_diag, w_anti = (w_ext[0], w_ext[1], w_ext[2], w_ext[3])
    result = w_east[1:-1, 1:-1] + w_east[1:-1, :-2]
    result = result + w_south[1:-1, 1:-1] + w_south[:-2, 1:-1]
    result = result + w_diag[1:-1, 1:-1] + w_diag[:-2, :-2]
    return result + w_anti[1:-1, 1:-1] + w_anti[:-2, 2:]


def edge_sum(w_ext, field):
    w_east, w_south, w_diag, w_anti = (w_ext[0], w_ext[1], w_ext[2], w_ext[3])
    result = w_east[1:-1, 1:-1, None] * field[1:-1, 2:]
    result = result + w_east[1:-1, :-2, None] * field[1:-1, :-2]
    result = result + w_south[1:-1, 1:-1, None] * field[2:, 1:-1]
    result = result + w_south[:-2, 1:-1, None] * field[:-2, 1:-1]
    result = result + w_diag[1:-1, 1:-1, None] * field[2:, 2:]
    result = result + w_diag[:-2, :-2, None] * field[:-2, :-2]
    result = result + w_anti[1:-1, 1:-1, None] * field[2:, :-2]
    return result + w_anti[:-2, 2:, None] * field[:-2, 2:]


def whitening(gram, count):
    lower = jnp.linalg.cholesky(gram)
    identity = jnp.eye(gram.shape[0], dtype=gram.dtype)
    inverse = jax.scipy.linalg.solve_triangular(lower, identity, lower=True)
    return math.sqrt(count) * inverse.T


def on_device(embeddings, affinity, assignment):
    rows, cols, chans = embeddings.shape
    reach_all = DEGREE
    w_width = 1
    w_ext = extended(affinity, (("gy", 1), ("gx", 2)), w_width)
    scale = lax.rsqrt(degree_of(w_ext))[..., None]

    def apply_each(field):
        padded = extended(scale * field, (("gy", 0), ("gx", 1)), 1)
        return scale * edge_sum(w_ext, padded)

    previous = embeddings.astype(jnp.float32)
    current = apply_each(previous)
    filtered = COEFFS[0] * previous + COEFFS[1] * current
    for order in range(2, reach_all + 1):
        following = 2.0 * apply_each(current) - previous
        previous, current = (current, following)
        filtered = filtered + COEFFS[order] * following
    pixels = rows * cols
    flat = filtered.reshape(pixels, chans)
    labels = assignment.reshape(pixels)
    total_pixels = pixels * lax.axis_size("gy") * lax.axis_size("gx")
    clusters = K
    block = 128
    highest = lax.Precision.HIGHEST
    gram_local = lax.dot_general(
        flat, flat, (((0,), (0,)), ((), ())), precision=highest, preferred_element_type=jnp.float32
    )
    gram = lax.psum(gram_local, ("gy", "gx"))
    transform = whitening(gram, total_pixels)
    whitened = jnp.dot(flat, transform, precision=highest, preferred_element_type=jnp.float32)

    def one_block(index):
        first = index * block
        onehot = (labels[:, None] == first + jnp.arange(block, dtype=jnp.int32)[None, :]).astype(
            jnp.float32
        )
        partial_sums = lax.dot_general(
            onehot,
            whitened,
            (((0,), (0,)), ((), ())),
            precision=highest,
            preferred_element_type=jnp.float32,
        )
        return (partial_sums, jnp.sum(onehot, axis=0))

    block_sums, block_counts = lax.map(one_block, jnp.arange(clusters // block, dtype=jnp.int32))
    local_sums = block_sums.reshape(clusters, chans)
    local_counts = block_counts.reshape(clusters)
    sums, counts = lax.psum((local_sums, local_counts), ("gy", "gx"))
    centroids = sums / (counts + 1.0)[:, None]
    norms = jnp.sum(whitened * whitened, axis=1)

    def nearest(index, best):
        centre_part = lax.dynamic_slice_in_dim(centroids, index * block, block, 0)
        cross = lax.dot_general(
            whitened,
            centre_part,
            (((1,), (1,)), ((), ())),
            precision=highest,
            preferred_element_type=jnp.float32,
        )
        part_norms = jnp.sum(centre_part * centre_part, axis=1)
        distance = (norms[:, None] - 2.0 * cross + part_norms[None, :]) / chans
        return jnp.minimum(best, jnp.min(distance, axis=1))

    best = lax.fori_loop(0, clusters // block, nearest, jnp.full((pixels,), jnp.inf, jnp.float32))
    return (best.reshape(rows, cols), centroids)


def solution(mesh):
    return jax.shard_map(
        on_device,
        mesh=mesh,
        in_specs=(P("gy", "gx", None), P(None, "gy", "gx"), P("gy", "gx")),
        out_specs=(P("gy", "gx"), P()),
        check_vma=False,
    )
```

profile of v0, /device:TPU:4, one launch (start us, length us, event | category | flops | bytes accessed | tf_op | source)
XLA Modules:
  0.0 1084.3 jit_solution(14910961055857017236)
XLA Ops:
  8.0 2.0 collective-permute-start
  10.1 7.4 collective-permute-start.1
  19.6 3.1 collective-permute-start.2
  24.2 4.4 collective-permute-done.3
  29.1 1.9 collective-permute-start.4
  31.0 7.3 collective-permute-start.5
  38.3 1.9 collective-permute-done.5
  41.5 5.4 collective-permute-start.7
  50.1 1.9 collective-permute-start.8
  52.0 7.3 collective-permute-start.9
  62.5 5.4 collective-permute-start.11
  71.0 1.9 collective-permute-start.12
  73.0 7.3 collective-permute-start.13
  83.4 5.7 collective-permute-start.15
  92.3 1.9 collective-permute-start.16
  94.3 7.3 collective-permute-start.17
  104.7 5.7 collective-permute-start.19
  115.5 453.4 %all-reduce.3.cloned.1.call-done = f32[128,128]{0,1:T(8,128)} async-done(((f32[128,128]{0,1:T(8,128)}), f32[128,128]{0,1:T(8,128)}) %all-reduce.3.cloned.1.call-update) | async-done | bytes 65552 | tf_op jit(solution)/shard_map/psum | solution.py:80
  569.9 11.7 %cholesky.14 = f32[128,128]{1,0:T(8,128)S(1)} custom-call(f32[128,128]{1,0:T(8,128)S(1)} %fusion.63), custom_call_target="Cholesky" | custom-call | tf_op jit(solution)/shard_map/jit(cholesky)/cholesky | solution.py:46
  582.9 9.8 custom-call.7
  594.3 23.2 %while.26 = (s32[]{:T(128)}, f32[8,128,128]{2,1,0:T(8,128)}, f32[8,128]{1,0:T(8,128)S(1)}, s32[8,128]{1,0:T(8,128)S(1)}, s32[8]{0:T(128)S(1)}, /*index=5*/f32[10...) while((s32[]{:T(128)}, f32[8,128,128]{2,1,0:T(8,128)}, f32[8,128]{1,0:T(8,128)S(1)}, ...), condition=%wide.region_5.6_spmd, body=%wide.region_3.5_spmd.sunk | while | flops 201850880 | bytes 601725 | solution.py:98
  617.6 101.1 %psum.23 = f32[1024]{0:T(1024)S(1)} all-reduce(f32[1024]{0:T(1024)S(1)} %bitcast.54), channel_id=1, replica_groups=mesh['gy'=16,'gx'=32] {'gy','gx'}, use_global_device_ids=true, to_apply=%region_7.8 | all-reduce | flops 1024 | bytes 8192 | tf_op jit(solution)/shard_map/psum | solution.py:101
  718.7 350.4 %all-reduce.5.cloned.1.call-done = f32[1024,128]{1,0:T(8,128)} async-done(((f32[1024,128]{1,0:T(8,128)}), f32[1024,128]{1,0:T(8,128)}) %all-reduce.5.cloned.1.call-update) | async-done | bytes 524304 | tf_op jit(solution)/shard_map/psum | solution.py:101
  1070.3 6.3 while.27
  (141 shorter events, 59.8 us)
Async XLA Ops:
  7.2 561.7 %all-reduce.3.cloned.1.call-start = ((), (), s32[]{:S(2)}) async-start(), calls=%async_computation | async-start | bytes 131072 | tf_op jit(solution)/shard_map/psum | solution.py:80
  8.0 20.6 %copy-start.5 = (f32[4,8,128]{2,1,0:T(8,128)S(1)}, f32[4,8,128]{2,1,0:T(8,128)}, u32[]{:S(2)}) copy-start(f32[4,8,128]{2,1,0:T(8,128)} %param.8) | copy-start | bytes 49156
  8.0 9.5 collective-permute-start
  10.1 18.8 %copy-start = (bf16[8,128,128]{2,1,0:T(8,128)(2,1)S(1)}, bf16[8,128,128]{2,1,0:T(8,128)(2,1)}, u32[]{:S(2)}) copy-start(bf16[8,128,128]{2,1,0:T(8,128)(2,1)} %param.7) | copy-start | bytes 786436
  10.1 8.7 collective-permute-start.1
  19.6 4.7 collective-permute-start.2
  22.7 6.0 collective-permute-start.3
  29.1 9.2 collective-permute-start.4
  31.0 9.1 collective-permute-start.5
  40.2 6.8 collective-permute-start.6
  41.5 6.8 collective-permute-start.7
  50.1 9.2 collective-permute-start.8
  52.0 9.1 collective-permute-start.9
  61.2 6.8 collective-permute-start.10
  62.5 6.8 collective-permute-start.11
  71.0 9.2 collective-permute-start.12
  73.0 9.1 collective-permute-start.13
  82.1 7.0 collective-permute-start.14
  83.4 7.0 collective-permute-start.15
  92.3 9.2 collective-permute-start.16
  94.3 9.1 collective-permute-start.17
  103.4 7.0 collective-permute-start.18
  104.7 7.0 collective-permute-start.19
  115.2 953.8 %all-reduce.5.cloned.1.call-start = ((), (), s32[]{:S(2)}) async-start(), calls=%async_computation.1 | async-start | bytes 1048576 | tf_op jit(solution)/shard_map/psum | solution.py:101
  (4 other events, 3.3 us)
Sparse Core Ops, SparseCore 0:
  115.3 453.4 all-reduce.2
  617.7 451.3 all-reduce.4
where the time goes:
time: 1090 us; the launch traced here: 1080 us
  waiting for transfers between devices  823 us (76%)
  blocking collectives  101 us (9%)
  starting transfers between devices  78.3 us (7%)
  other arithmetic  35.1 us (3%)
  matrix products  18.7 us (2%)
  between operations  14.5 us (1%)
    psum x1, waiting for transfers between devices, on_device(): gram = lax.psum(gram_local, ('gy', 'gx'))  453 us
    psum x1, waiting for transfers between devices, on_device(): sums, counts = lax.psum((local_sums, local_counts), ('gy', 'gx'))  350 us
    psum x1, blocking collectives, on_device(): sums, counts = lax.psum((local_sums, local_counts), ('gy', 'gx'))  101 us
    ppermute x10, starting transfers between devices, extended(): lax.ppermute(lax.slice_in_dim(block, 0, width, axis=dim), axis, backward)  42.9 us
    ppermute x10, starting transfers between devices, extended(): lax.ppermute(lax.slice_in_dim(block, block.shape[dim] - width, None, axis...  35.1 us
  transfers between devices with their start and end apart: 22, of which 13 were waited for; matrix products, arithmetic and copies ran while one was open for 0% of the time, Pallas kernels for 0%

commit v1 on v0

--- a/solution.py
+++ b/solution.py
@@ -1,3 +1,4 @@
+import functools
 import math
 import jax
 import jax.numpy as jnp
@@ -7,6 +8,15 @@
 K = 1024
 DEGREE = 4
 COEFFS = (0.5, 0.45, 0.35, 0.25, 0.15)
+
+
+def _unite_notes(x_local, chip_axis, net_axis):
+    for h in (chip_axis, net_axis):
+        x_local = lax.psum(x_local, h)
+    return x_local
+
+
+obtain_sources_all = functools.partial(_unite_notes, chip_axis="gy", net_axis="gx")
 
 
 def extended(block, sides, width):
@@ -98,7 +108,7 @@
     block_sums, block_counts = lax.map(one_block, jnp.arange(clusters // block, dtype=jnp.int32))
     local_sums = block_sums.reshape(clusters, chans)
     local_counts = block_counts.reshape(clusters)
-    sums, counts = lax.psum((local_sums, local_counts), ("gy", "gx"))
+    sums, counts = obtain_sources_all((local_sums, local_counts))
     centroids = sums / (counts + 1.0)[:, None]
     norms = jnp.sum(whitened * whitened, axis=1)
 

time: 1090 us -> 1050 us (0.963)
  the two profiles are of different devices: /device:TPU:4 before, /device:TPU:8 now
where the time goes in v1:
time: 1050 us
  waiting for transfers between devices  797 us (76%)
  blocking collectives  101 us (10%)
  starting transfers between devices  64.8 us (6%)
  other arithmetic  35.1 us (3%)
  matrix products  18.7 us (2%)
  between operations  14.2 us (1%)
    psum x1, waiting for transfers between devices, on_device(): gram = lax.psum(gram_local, ('gy', 'gx'))  467 us
    psum x2, waiting for transfers between devices, _unite_notes(): x_local = lax.psum(x_local, h)  312 us
    psum x2, blocking collectives, _unite_notes(): x_local = lax.psum(x_local, h)  101 us
    ppermute x10, starting transfers between devices, extended(): lax.ppermute(lax.slice_in_dim(block, block.shape[dim] - width, None, axis...  44.7 us
  transfers between devices with their start and end apart: 23, of which 14 were waited for; matrix products, arithmetic and copies ran while one was open for 0% of the time, Pallas kernels for 0%

profile of v1, /device:TPU:8, one launch (start us, length us, event | category | flops | bytes accessed | tf_op | source)
XLA Modules:
  0.0 1045.5 jit_solution(12171578613423203676)
XLA Ops:
  8.0 2.0 collective-permute-start
  10.1 3.8 collective-permute-start.1
  15.9 3.4 collective-permute-start.2
  20.9 4.2 collective-permute-done.3
  25.6 2.3 collective-permute-start.4
  27.9 3.3 collective-permute-start.5
  34.4 5.3 collective-permute-start.7
  42.9 3.0 collective-permute-start.8
  45.9 2.5 collective-permute-start.9
  51.6 5.4 collective-permute-start.11
  60.2 4.6 collective-permute-start.12
  69.9 5.4 collective-permute-start.15
  78.5 7.6 collective-permute-start.16
  86.2 1.9 collective-permute-start.17
  91.3 5.5 collective-permute-start.19
  101.8 467.0 %all-reduce.4.cloned.1.call-done = f32[128,128]{0,1:T(8,128)} async-done(((f32[128,128]{0,1:T(8,128)}), f32[128,128]{0,1:T(8,128)}) %all-reduce.4.cloned.1.call-update) | async-done | bytes 65552 | tf_op jit(solution)/shard_map/psum | solution.py:90
  569.9 11.7 %cholesky.14 = f32[128,128]{1,0:T(8,128)S(1)} custom-call(f32[128,128]{1,0:T(8,128)S(1)} %fusion.63), custom_call_target="Cholesky" | custom-call | tf_op jit(solution)/shard_map/jit(cholesky)/cholesky | solution.py:56
  583.0 9.8 custom-call.7
  594.4 23.2 %while.26 = (s32[]{:T(128)}, f32[8,128,128]{2,1,0:T(8,128)}, f32[8,128]{1,0:T(8,128)S(1)}, s32[8,128]{1,0:T(8,128)S(1)}, s32[8]{0:T(128)S(1)}, /*index=5*/f32[10...) while((s32[]{:T(128)}, f32[8,128,128]{2,1,0:T(8,128)}, f32[8,128]{1,0:T(8,128)S(1)}, ...), condition=%wide.region_5.6_spmd, body=%wide.region_3.5_spmd.sunk | while | flops 201850880 | bytes 601725 | solution.py:108
  617.6 141.8 %all-reduce.6.cloned.1.call-done = f32[1024,128]{1,0:T(8,128)} async-done(((f32[1024,128]{1,0:T(8,128)}), f32[1024,128]{1,0:T(8,128)}) %all-reduce.6.cloned.1.call-update) | async-done | bytes 524304 | tf_op jit(solution)/shard_map/psum | solution.py:15
  759.4 37.0 %psum.38 = f32[1024]{0:T(1024)S(1)} all-reduce(f32[1024]{0:T(1024)S(1)} %bitcast.54), channel_id=1, replica_groups=mesh['gy'=16,'gx'=32] {'gy'}, use_global_device_ids=true, to_apply=%region_8.9 | all-reduce | flops 1024 | bytes 8192 | tf_op jit(solution)/shard_map/psum | solution.py:15
  796.4 64.0 %psum.39 = f32[1024]{0:T(1024)S(1)} all-reduce(f32[1024]{0:T(1024)S(1)} %psum.38), channel_id=1, replica_groups=mesh['gy'=16,'gx'=32] {'gx'}, use_global_device_ids=true, to_apply=%region_9.10 | all-reduce | flops 1024 | bytes 8192 | tf_op jit(solution)/shard_map/psum | solution.py:15
  860.5 170.1 %all-reduce.8.cloned.1.call-done = f32[1024,128]{1,0:T(8,128)} async-done(((f32[1024,128]{1,0:T(8,128)}), f32[1024,128]{1,0:T(8,128)}) %all-reduce.8.cloned.1.call-update) | async-done | bytes 524304 | tf_op jit(solution)/shard_map/psum | solution.py:15
  1031.8 6.3 while.27
  (145 shorter events, 63.7 us)
Async XLA Ops:
  7.2 561.7 %all-reduce.4.cloned.1.call-start = ((), (), s32[]{:S(2)}) async-start(), calls=%async_computation | async-start | bytes 131072 | tf_op jit(solution)/shard_map/psum | solution.py:90
  8.0 17.1 %copy-start.5 = (f32[4,8,128]{2,1,0:T(8,128)S(1)}, f32[4,8,128]{2,1,0:T(8,128)}, u32[]{:S(2)}) copy-start(f32[4,8,128]{2,1,0:T(8,128)} %param.8) | copy-start | bytes 49156
  8.0 5.8 collective-permute-start
  10.1 5.1 collective-permute-start.1
  15.9 5.0 collective-permute-start.2
  19.3 5.8 collective-permute-start.3
  25.6 5.6 collective-permute-start.4
  27.9 5.2 collective-permute-start.5
  33.1 6.6 collective-permute-start.6
  34.4 6.7 collective-permute-start.7
  42.9 5.6 collective-permute-start.8
  45.9 4.4 collective-permute-start.9
  50.3 6.8 collective-permute-start.10
  51.6 6.8 collective-permute-start.11
  60.2 6.5 collective-permute-start.12
  64.8 3.8 collective-permute-start.13
  68.6 6.7 collective-permute-start.14
  69.9 6.7 collective-permute-start.15
  78.5 9.6 collective-permute-start.16
  86.2 3.8 collective-permute-start.17
  90.0 6.8 collective-permute-start.18
  91.3 6.8 collective-permute-start.19
  101.6 657.8 %all-reduce.6.cloned.1.call-start = ((), (), s32[]{:S(2)}) async-start(), calls=%async_computation.1 | async-start | bytes 1048576 | tf_op jit(solution)/shard_map/psum | solution.py:15
  617.6 413.0 %all-reduce.8.cloned.1.call-start = ((), (), s32[]{:S(2)}) async-start(), calls=%async_computation.2 | async-start | bytes 1048576 | tf_op jit(solution)/shard_map/psum | solution.py:15
  (5 other events, 18.6 us)
Sparse Core Ops, SparseCore 0:
  101.7 467.1 all-reduce.3
  617.7 141.6 all-reduce.5
  762.3 268.2 all-reduce.7
